TPU v7x, 512 devices: a whole 4x8x8 slice. The times are simulated.
512 devices in a mesh: section: 16 (over x_lo, z), latent: 32 (over x_hi, y, core).
Axes of the slice: x: 4 (x_hi: 2, x_lo: 2; x = x_hi * 2 + x_lo), y: 8, z: 8, core: 2. Of those that a mesh axis runs over, the one named last changes fastest.
Arguments:
- residual: bfloat16 [4, 320, 4608], P(None, None, 'latent'), may hold values from -6 to 6
- encoder: bfloat16 [16, 4608, 4096], P('section', None, 'latent'), may hold values from -0.09375 to 0.09375
- enc_bias: float32 [16, 4096], P('section', 'latent'), may hold values from -4 to 4
- gate_code: int32 [16, 4096], P('section', 'latent'), may hold values from 0 to 2
- decoder: bfloat16 [16, 3, 4096, 4608], P('section', None, 'latent'), may hold values from -0.0546875 to 0.0546875
Outputs:
- reconstruction: bfloat16 [16, 80, 4608], P('section', None, 'latent')
- latent_acts: bfloat16 [16, 320, 4096], P('section', None, 'latent')
Inputs may be any that keep to these rules, and one draw needn't show every extreme that they name: `gate_code`: 0: the latent is always active; 1: its threshold is zero; 2: it is never active.
All inputs are finite; a program needn't handle non-finite values.
Results may differ from a plain program's by a relative error of at most 0.019.
Values may be sent and summed in bfloat16 or wider, within the bound.
A program may use at most 64 MiB of HBM per device.

v0:
```python
import jax
import jax.numpy as jnp
from jax import lax
from jax.sharding import PartitionSpec as P

LAYERS = 4


def swapped(shard, axis, stride):
    return lax.ppermute(shard, axis, [(i, i ^ 1 << stride) for i in range(lax.axis_size(axis))])


def passed_along(value, axis, steps):
    count = lax.axis_size(axis)
    first, last = (max(0, -steps), min(count, count - steps))
    return lax.ppermute(value, axis, [(source, source + steps) for source in range(first, last)])


def group_reduce(partial_rows, group_size):
    current = partial_rows
    section_index = lax.axis_index("section")
    level_count = group_size.bit_length() - 1
    for level in reversed(range(level_count)):
        half = current.shape[0] // 2
        lower = current[:half]
        upper = current[half:]
        high_side = section_index // 2**level % 2 == 1
        kept = jnp.where(high_side, upper, lower)
        sent = jnp.where(high_side, lower, upper)
        received = swapped(sent.astype(jnp.bfloat16), "section", level).astype(sent.dtype)
        current = kept + received
    return current


def shards(residual, encoder, enc_bias, gate_code, decoder):
    group_size = lax.axis_size("section") // LAYERS
    layer_index = lax.axis_index("section") // group_size
    resid_layer = lax.dynamic_index_in_dim(residual, layer_index, 0, keepdims=False)
    enc_local = encoder[0]
    preact = jnp.dot(
        lax.all_gather(resid_layer, "latent", axis=1, tiled=True),
        enc_local,
        preferred_element_type=jnp.float32,
    )
    preact = preact + enc_bias[0]
    threshold = 10000.0 * (gate_code[0].astype(jnp.float32) - 1.0)
    active_vals = jnp.where(preact > threshold, preact, jnp.zeros_like(preact)).astype(jnp.bfloat16)
    reach_count = decoder.shape[1]
    sources = [active_vals]
    carried = active_vals
    for hop_index in range(1, reach_count):
        carried = passed_along(carried, "section", group_size)
        sources.append(carried)
    stacked = jnp.stack(sources, axis=0)
    dec_local = decoder[0]
    own_share = lax.psum_scatter(
        lax.dot_general(
            dec_local, stacked, (((0, 1), (0, 2)), ((), ())), preferred_element_type=jnp.float32
        ).astype(jnp.bfloat16),
        "latent",
        scatter_dimension=0,
        tiled=True,
    ).astype(jnp.float32)
    summed = jnp.transpose(own_share)
    rebuilt = group_reduce(summed, group_size).astype(jnp.bfloat16)
    return (rebuilt[None], active_vals[None])


def solution(mesh):
    return jax.shard_map(
        shards,
        mesh=mesh,
        in_specs=(
            P(None, None, "latent"),
            P("section", None, "latent"),
            P("section", "latent"),
            P("section", "latent"),
            P("section", None, "latent", None),
        ),
        out_specs=(P("section", None, "latent"), P("section", None, "latent")),
        check_vma=False,
    )
```

profile of v0, /device:TPU:16, one launch (start us, length us, event | category | flops | bytes accessed | tf_op | source)
XLA Modules:
  0.0 296.9 jit_solution(9694946097347359255)
XLA Ops:
  7.2 0.0 copy-start
  7.2 0.0 all-gather.3.cloned.1.call-start
  7.2 1.7 constant_dynamic-slice_fusion
  8.9 0.0 all-gather.3.cloned.1.call-update
  9.0 0.0 reduce-scatter.4.cloned.1.call-start
  9.0 0.7 multiply_bitcast_fusion
  9.7 94.1 %all-gather.3.cloned.1.call-done = bf16[1,320,4608]{1,2,0:T(8,128)(2,1)} async-done(((bf16[1,320,144]{1,2,0:T(8,128)(2,1)}), bf16[1,320,4608]{1,2,0:T(8,128)(2,1)}) %all-gather.3.cloned.1.call-update) | async-done | bytes 2949136 | tf_op jit(solution)/shard_map/all_gather | solution.py:41
  103.8 3.5 %fusion.15 = bf16[320,128]{1,0:T(8,128)(2,1)S(1)} fusion(bf16[1,4608,128]{2,1,0:T(8,128)(2,1)} %param.6, bf16[1,320,4608]{1,2,0:T(8,128)(2,1)} %all-gather.3.cloned.1.call-done, f32[128]{0:T(128)S(1)} %multiply_bitcast_fusion, f32[128]{0:T(128)} %bitcast.44), kind=kOutput, calls=%fused_computation.9 | convolution fusion | flops 377651200 | bytes 4211712 | tf_op jit(solution)/shard_map/dot_general | solution.py:40
  107.3 0.0 copy-start.2
  107.3 8.0 %collective-permute-start = (bf16[320,128]{1,0:T(8,128)(2,1)S(1)}, bf16[320,128]{1,0:T(8,128)(2,1)S(1)}, u32[]{:S(2)}, u32[]{:S(2)}) collective-permute-start(bf16[320,128]{1,0:T(8,128)(2,1)S(1)} %fusion.15), channel_id=1, source_target_pairs={{0,128},{32,160},{64,192},{96,224},{128,256},{160,288},{192,320},{... | collective-permute-start | bytes 245768 | tf_op jit(solution)/shard_map/ppermute | solution.py:16
  115.3 2.1 collective-permute-done
  117.5 9.9 %collective-permute-start.1 = (bf16[320,128]{1,0:T(8,128)(2,1)S(1)}, bf16[320,128]{1,0:T(8,128)(2,1)S(1)}, u32[]{:S(2)}, u32[]{:S(2)}) collective-permute-start(bf16[320,128]{1,0:T(8,128)(2,1)S(1)} %collective-permute-done), channel_id=1, source_target_pairs={{0,128},{32,160},{64,192},{96,224},{128,256},{160,288},{192,320},{... | collective-permute-start | bytes 245768 | tf_op jit(solution)/shard_map/ppermute | solution.py:16
  127.3 3.7 %collective-permute-done.1 = bf16[320,128]{1,0:T(8,128)(2,1)S(1)} collective-permute-done((bf16[320,128]{1,0:T(8,128)(2,1)S(1)}, bf16[320,128]{1,0:T(8,128)(2,1)S(1)}, u32[]{:S(2)}, u32[]{:S(2)}) %collective-permute-start.1) | collective-permute-done | bytes 81952 | tf_op jit(solution)/shard_map/ppermute | solution.py:16
  131.0 0.0 copy-done.2
  131.0 0.0 copy-done
  131.0 3.3 %fusion.1 = bf16[4608,320]{0,1:T(8,128)(2,1)} fusion(bf16[1,3,128,4608]{3,2,1,0:T(8,128)(2,1)S(1)} %copy-done, bf16[1,320,128]{2,1,0:T(8,128)(2,1)S(1)} %bitcast.43, bf16[1,320,128]{2,1,0:T(8,128)(2,1)S(1)} %bitcast.42, bf16[1,320,128]{2,1,0:T(8,128)(2,1)S(1)} %bitcast.40), kind=kOutput, calls=%fused_computation.2 | convolution fusion | flops 1134182400 | bytes 6733824 | tf_op jit(solution)/shard_map/dot_general | solution.py:57
  134.3 5.5 %copy.9 = bf16[4608,320]{1,0:T(8,128)(2,1)} copy(bf16[4608,320]{0,1:T(8,128)(2,1)} %fusion.1) | data formatting | bytes 5898240
  139.8 0.0 reduce-scatter.4.cloned.1.call-update
  139.9 129.5 %reduce-scatter.4.cloned.1.call-done = bf16[144,320]{1,0:T(8,128)(2,1)} async-done(((bf16[4608,320]{1,0:T(8,128)(2,1)}), bf16[144,320]{1,0:T(8,128)(2,1)}) %reduce-scatter.4.cloned.1.call-update) | async-done | bytes 92176
  269.4 1.7 copy.10
  271.0 0.9 convert_bitcast_fusion
  272.0 0.0 copy-start.1
  272.0 0.7 copy-done.1
  272.7 0.7 select_convert_fusion
  273.4 4.6 %collective-permute-start.2 = (bf16[160,144]{1,0:T(8,128)(2,1)}, bf16[160,144]{1,0:T(8,128)(2,1)}, u32[]{:S(2)}, u32[]{:S(2)}) collective-permute-start(bf16[160,144]{1,0:T(8,128)(2,1)} %select_convert_fusion), channel_id=1, source_target_pairs={{0,64},{32,96},{64,0},{96,32},{128,192},{160,224},{192,128},{224,1... | collective-permute-start | bytes 138248 | tf_op jit(solution)/shard_map/ppermute | solution.py:10
  278.0 2.9 collective-permute-done.2
  280.9 1.1 convert_add_fusion
  282.0 3.6 %collective-permute-start.3 = (bf16[80,144]{1,0:T(8,128)(2,1)S(1)}, bf16[80,144]{1,0:T(8,128)(2,1)S(1)}, u32[]{:S(2)}, u32[]{:S(2)}) collective-permute-start(bf16[80,144]{1,0:T(8,128)(2,1)S(1)} %select_convert_fusion.1), channel_id=1, source_target_pairs={{0,32},{32,0},{64,96},{96,64},{128,160},{160,128},{192,224},{224,1... | collective-permute-start | bytes 69128 | tf_op jit(solution)/shard_map/ppermute | solution.py:10
  285.6 2.3 collective-permute-done.3
  287.9 0.6 fusion.25
  288.5 1.5 copy.8
  (1 shorter events, 0.0 us)
Async XLA Ops:
  7.2 123.9 %copy-start = (bf16[1,3,128,4608]{3,2,1,0:T(8,128)(2,1)S(1)}, bf16[1,3,128,4608]{3,2,1,0:T(8,128)(2,1)}, u32[]{:S(2)}) copy-start(bf16[1,3,128,4608]{3,2,1,0:T(8,128)(2,1)} %param.9) | copy-start | bytes 10616836
  7.2 96.6 %all-gather.3.cloned.1.call-start = ((), (), s32[]{:S(2)}) async-start(), calls=%async_computation.1 | async-start | bytes 3649536 | tf_op jit(solution)/shard_map/all_gather | solution.py:41
  9.0 260.4 %reduce-scatter.4.cloned.1.call-start = ((), (), s32[]{:S(2)}) async-start(), calls=%async_computation.2 | async-start | bytes 3649536
  107.3 23.7 %copy-start.2 = (bf16[320,128]{1,0:T(8,128)(2,1)}, bf16[320,128]{1,0:T(8,128)(2,1)S(1)}, u32[]{:S(2)}) copy-start(bf16[320,128]{1,0:T(8,128)(2,1)S(1)} %fusion.15) | copy-start | bytes 245764
  107.3 10.2 %collective-permute-start = (bf16[320,128]{1,0:T(8,128)(2,1)S(1)}, bf16[320,128]{1,0:T(8,128)(2,1)S(1)}, u32[]{:S(2)}, u32[]{:S(2)}) collective-permute-start(bf16[320,128]{1,0:T(8,128)(2,1)S(1)} %fusion.15), channel_id=1, source_target_pairs={{0,128},{32,160},{64,192},{96,224},{128,256},{160,288},{192,320},{... | collective-permute-start | bytes 245768 | tf_op jit(solution)/shard_map/ppermute | solution.py:16
  117.5 13.6 %collective-permute-start.1 = (bf16[320,128]{1,0:T(8,128)(2,1)S(1)}, bf16[320,128]{1,0:T(8,128)(2,1)S(1)}, u32[]{:S(2)}, u32[]{:S(2)}) collective-permute-start(bf16[320,128]{1,0:T(8,128)(2,1)S(1)} %collective-permute-done), channel_id=1, source_target_pairs={{0,128},{32,160},{64,192},{96,224},{128,256},{160,288},{192,320},{... | collective-permute-start | bytes 245768 | tf_op jit(solution)/shard_map/ppermute | solution.py:16
  272.0 0.7 copy-start.1
  273.4 7.5 %collective-permute-start.2 = (bf16[160,144]{1,0:T(8,128)(2,1)}, bf16[160,144]{1,0:T(8,128)(2,1)}, u32[]{:S(2)}, u32[]{:S(2)}) collective-permute-start(bf16[160,144]{1,0:T(8,128)(2,1)} %select_convert_fusion), channel_id=1, source_target_pairs={{0,64},{32,96},{64,0},{96,32},{128,192},{160,224},{192,128},{224,1... | collective-permute-start | bytes 138248 | tf_op jit(solution)/shard_map/ppermute | solution.py:10
  282.0 5.9 %collective-permute-start.3 = (bf16[80,144]{1,0:T(8,128)(2,1)S(1)}, bf16[80,144]{1,0:T(8,128)(2,1)S(1)}, u32[]{:S(2)}, u32[]{:S(2)}) collective-permute-start(bf16[80,144]{1,0:T(8,128)(2,1)S(1)} %select_convert_fusion.1), channel_id=1, source_target_pairs={{0,32},{32,0},{64,96},{96,64},{128,160},{160,128},{192,224},{224,1... | collective-permute-start | bytes 69128 | tf_op jit(solution)/shard_map/ppermute | solution.py:10
Sparse Core Ops, SparseCore 0:
  11.3 92.4 all-gather.2
  140.0 129.3 reduce-scatter.3
where the time goes:
time: 297 us
  waiting for transfers between devices  235 us (79%)
  starting transfers between devices  26.2 us (9%)
  between operations  14.2 us (5%)
  local copies, waits for them, and re-layouts  11.1 us (4%)
  matrix products  6.78 us (2%)
  other arithmetic  3.95 us (1%)
    unnamed x3, waiting for transfers between devices  130 us
    all_gather x1, waiting for transfers between devices, shards(): lax.all_gather(resid_layer, 'latent', axis=1, tiled=True)  94.1 us
    ppermute x2, starting transfers between devices, passed_along(): lax.ppermute(value, axis, [(source, source + steps) for source in range(f...  17.9 us
    unnamed x9, local copies, waits for them, and re-layouts  9.42 us
    ppermute x2, starting transfers between devices, swapped(): lax.ppermute(shard, axis, [(i, i ^ 1 << stride) for i in range(lax.axis_s...  8.22 us
  transfers between devices with their start and end apart: 6, of which 6 were waited for; matrix products, arithmetic and copies ran while one was open for 0% of the time, Pallas kernels for 0%

commit v1 on v0

v1 whole, which is shorter than its diff:
```python
import jax
import jax.numpy as jnp
from jax import lax
from jax.experimental import pallas as pl
from jax.experimental.pallas import tpu as pltpu
from jax.sharding import PartitionSpec as P

MESH = pl.DeviceIdType.MESH
BF16 = jnp.bfloat16
F32 = jnp.float32

NY = 8
GROUP = 4
OFFSETS = (4, 3, -3, 2, -2, 1, -1, 0)
PLACE = {offset: place for place, offset in enumerate(OFFSETS)}
PLACE[-4] = PLACE[4]


def kernel(
    resid, enc, bias, gate, dec, rec_out, act_out,
    gathered, enc_v, dec_v, enc_t, dec_t, acts_in, acts_all, shares, sibling_in, ring, own_sum, final_out, final_in,
    load_sem, local_sem, cross_send, cross_recv, gather_send, gather_recv, pair_send, pair_recv,
    act_send, act_recv, share_send, share_recv, ring_send, ring_recv, final_send, final_recv,
):
    width, tokens = gathered.shape[3:]
    section = lax.axis_index("section")
    latent = lax.axis_index("latent")
    x_lo, z = section // 8, section % 8
    x_hi, y, core = latent // 16, latent // 2 % 8, latent % 2
    layer, g = section // GROUP, section % GROUP

    def device(section_index, hi, y_index, core_index):
        return (section_index, hi * 16 + y_index * 2 + core_index)

    up = device(section, x_hi, (y + 1) % NY, core)
    down = device(section, x_hi, (y + NY - 1) % NY, core)
    sibling = device(section, x_hi, y, 1 - core)
    across = device((1 - x_lo) * 8 + z, 1 - x_hi, y, core)
    later = [((section + 4) % 16, latent), ((section + 8) % 16, latent)]
    peers = []
    for code in range(1, 8):
        flip_x, flip_g = code // 4, code % 4
        hi = 1 - x_hi if flip_x else x_hi
        low, high = g % 2, g // 2
        low = 1 - low if flip_g % 2 else low
        high = 1 - high if flip_g // 2 else high
        peer_g = high * 2 + low
        peers.append((hi, peer_g, device(section - g + peer_g, hi, y, core)))

    partners = [up, down, sibling, across, later[0], later[1], ((section + 12) % 16, latent)]
    partners += [peer[2] for peer in peers]
    barrier = pltpu.get_barrier_semaphore()
    for partner in partners:
        pl.semaphore_signal(barrier, inc=1, device_id=partner, device_id_type=MESH)
    loads = [
        pltpu.make_async_copy(enc, enc_v, load_sem.at[0]),
        pltpu.make_async_copy(dec, dec_v, load_sem.at[1]),
    ]
    for load in loads:
        load.start()
    local = pltpu.make_async_copy(resid.at[layer], gathered.at[x_hi, y, core], local_sem)
    local.start()
    local.wait()
    pl.semaphore_wait(barrier, len(partners))

    def remote(source, target, send, recv, to):
        copy = pltpu.make_async_remote_copy(
            src_ref=source, dst_ref=target, send_sem=send, recv_sem=recv, device_id=to, device_id_type=MESH
        )
        copy.start()
        return copy

    pending = []
    half = (x_hi, 1 - x_hi)
    crossed = remote(
        resid.at[(1 - x_lo) * 2 + z // 4], gathered.at[x_hi, y, core], cross_send, cross_recv, across
    )
    gather = {}
    pairs = {}

    def send_gather(step, way, q):
        origin = (y + (NY - step if way == 0 else step)) % NY
        block = gathered.at[half[q], origin, core]
        gather[step, way, q] = remote(
            block, block, gather_send.at[step, way, q], gather_recv.at[step, way, q], up if way == 0 else down
        )

    def send_pair(offset, q):
        origin = (y + (offset + NY) % NY) % NY
        block = gathered.at[half[q], origin, core]
        place = PLACE[offset]
        pairs[place, q] = remote(block, block, pair_send.at[place, q], pair_recv.at[place, q], sibling)

    for way in range(2):
        send_gather(0, way, 0)
    send_pair(0, 0)

    loads[0].wait()

    def turn_encoder(block, carry):
        rows = pl.ds(pl.multiple_of(block * 2 * width, 16), 2 * width)
        enc_t[block] = jnp.transpose(enc_v[0, rows, :])
        return carry

    lax.fori_loop(0, 16, turn_encoder, 0)
    crossed.wait_recv()
    for way in range(2):
        send_gather(0, way, 1)
    send_pair(0, 1)
    loads[1].wait()

    def turn_decoder(block, carry):
        columns = pl.ds(pl.multiple_of(block * 128, 128), 128)
        for k in range(3):
            dec_t[columns, k * 128 : (k + 1) * 128] = jnp.transpose(dec_v[0, k, :, columns])
        return carry

    lax.fori_loop(0, 36, turn_decoder, 0)

    def encoded(offset):
        origin = (y + (offset + NY) % NY) % NY
        for q in range(2):
            pairs[PLACE[offset], q].wait_recv()

        def one(hi, total):
            block = gathered[hi, origin].reshape(2 * width, tokens)
            return total + jnp.dot(enc_t[hi * NY + origin], block, preferred_element_type=F32)

        return lax.fori_loop(0, 2, one, jnp.zeros((128, tokens), F32))

    preact_t = None
    for step in range(4):
        for q in range(2):
            for way in range(2):
                if (step, way, q) not in gather:
                    continue
                gather[step, way, q].wait_recv()
                if step < 2 or (step == 2 and way == q):
                    send_gather(step + 1, way, q)
                send_pair((step + 1) * (-1 if way == 0 else 1), q)
        for offset in ((0,) if step == 0 else (step, -step)):
            term = encoded(offset)
            preact_t = term if preact_t is None else preact_t + term
    preact_t = preact_t + encoded(4)
    preact = jnp.transpose(preact_t) + bias[...]
    threshold = 10000.0 * (gate[...].astype(F32) - 1.0)
    acts = jnp.where(preact > threshold, preact, jnp.zeros_like(preact)).astype(BF16)
    act_out[0] = acts
    acts_all[:, 0:128] = acts
    passed = [
        remote(act_out.at[0], acts_in.at[k], act_send.at[k], act_recv.at[k], later[k]) for k in (1, 0)
    ][::-1]
    for k in (1, 0):
        passed[k].wait_recv()
        arrived = acts_in[k]
        acts_all[:, (k + 1) * 128 : (k + 2) * 128] = jnp.where(layer > k, arrived, jnp.zeros_like(arrived))

    share_copies = {}

    def decode(place):
        target = (y + (OFFSETS[place] + NY) % NY) % NY

        def one(hi, carry):
            rows = pl.ds(pl.multiple_of((hi * NY + target) * 2 * width, 16), 2 * width)
            product = lax.dot_general(
                dec_t[rows, :], acts_all[...], (((1,), (1,)), ((), ())), preferred_element_type=F32
            )
            shares[place, hi] = product.astype(BF16).reshape(2, width, tokens)
            return carry

        lax.fori_loop(0, 2, one, 0)
        for hi in range(2):
            share_copies[place, hi] = remote(
                shares.at[place, hi, 1 - core],
                sibling_in.at[place, hi],
                share_send.at[place, hi],
                share_recv.at[place, hi],
                sibling,
            )

    def chip_sum(place, hi):
        share_copies[place, hi].wait_recv()
        return shares[place, hi, core].astype(F32) + sibling_in[place, hi].astype(F32)

    ring_copies = {}

    def send_ring(way, distance, hi):
        ring_copies[way, distance, hi] = remote(
            ring.at[way, distance, hi],
            ring.at[way, distance - 1, hi],
            ring_send.at[way, distance, hi],
            ring_recv.at[way, distance, hi],
            up if way == 0 else down,
        )

    def add_ring(way, distance, hi):
        place = PLACE[distance if way == 0 else -distance]
        total = chip_sum(place, hi)
        if (way, distance + 1, hi) in ring_copies:
            ring_copies[way, distance + 1, hi].wait_recv()
            total = total + ring[way, distance, hi].astype(F32)
        ring[way, distance, hi] = total.astype(BF16)
        send_ring(way, distance, hi)

    decode(0)
    decode(1)
    for way in range(2):
        add_ring(way, 4, way)
    decode(2)
    for way in range(2):
        add_ring(way, 3, 1 - way)
    decode(3)
    decode(4)
    for way in range(2):
        add_ring(way, 3, way)
    decode(5)
    decode(6)
    for way in range(2):
        add_ring(way, 2, 1 - way)
    decode(7)
    for way in range(2):
        add_ring(way, 2, way)
    for hi in range(2):
        for way in range(2):
            add_ring(way, 1, hi if way == 1 else 1 - hi)
    for hi in range(2):
        total = chip_sum(7, hi)
        for way in range(2):
            ring_copies[way, 1, hi].wait_recv()
            total = total + ring[way, 0, hi].astype(F32)
        turned = jnp.transpose(total).reshape(GROUP, tokens // GROUP, width)
        own_sum[hi] = turned
        final_out[hi] = turned.astype(BF16)
    finals = [
        remote(final_out.at[hi, peer_g], final_in.at[i], final_send.at[i], final_recv.at[i], to)
        for i, (hi, peer_g, to) in enumerate(peers)
    ]
    total = own_sum[x_hi, g]
    for i, copy in enumerate(finals):
        copy.wait_recv()
        total = total + final_in[i].astype(F32)
    rec_out[0] = total.astype(BF16)

    for group in ([crossed], gather.values(), pairs.values(), passed, share_copies.values(), ring_copies.values(), finals):
        for copy in group:
            copy.wait_send()


def shards(residual, encoder, enc_bias, gate_code, decoder):
    layers, tokens, width = residual.shape
    model = encoder.shape[1]
    vmem = pl.BlockSpec(memory_space=pltpu.VMEM)
    hbm = pl.BlockSpec(memory_space=pl.ANY)
    dma = pltpu.SemaphoreType.DMA
    return pl.pallas_call(
        kernel,
        out_shape=(
            jax.ShapeDtypeStruct((1, tokens // GROUP, width), BF16),
            jax.ShapeDtypeStruct((1, tokens, 128), BF16),
        ),
        in_specs=[vmem, hbm, vmem, vmem, hbm],
        out_specs=(vmem, vmem),
        scratch_shapes=[
            pltpu.VMEM((2, NY, 2, width, tokens), BF16),
            pltpu.VMEM((1, model, 128), BF16),
            pltpu.VMEM((1, 3, 128, model), BF16),
            pltpu.VMEM((16, 128, 2 * width), BF16),
            pltpu.VMEM((model, 384), BF16),
            pltpu.VMEM((2, tokens, 128), BF16),
            pltpu.VMEM((tokens, 384), BF16),
            pltpu.VMEM((8, 2, 2, width, tokens), BF16),
            pltpu.VMEM((8, 2, width, tokens), BF16),
            pltpu.VMEM((2, 5, 2, width, tokens), BF16),
            pltpu.VMEM((2, GROUP, tokens // GROUP, width), F32),
            pltpu.VMEM((2, GROUP, tokens // GROUP, width), BF16),
            pltpu.VMEM((7, tokens // GROUP, width), BF16),
            dma((2,)),
            dma(()),
            dma(()),
            dma(()),
            dma((4, 2, 2)),
            dma((4, 2, 2)),
            dma((8, 2)),
            dma((8, 2)),
            dma((2,)),
            dma((2,)),
            dma((8, 2)),
            dma((8, 2)),
            dma((2, 5, 2)),
            dma((2, 5, 2)),
            dma((7,)),
            dma((7,)),
        ],
        compiler_params=pltpu.CompilerParams(
            collective_id=0, has_side_effects=True, vmem_limit_bytes=48 * 1024 * 1024
        ),
    )(jnp.transpose(residual, (0, 2, 1)), encoder, enc_bias, gate_code, decoder)


def solution(mesh):
    return jax.shard_map(
        shards,
        mesh=mesh,
        in_specs=(
            P(None, None, "latent"),
            P("section", None, "latent"),
            P("section", "latent"),
            P("section", "latent"),
            P("section", None, "latent", None),
        ),
        out_specs=(P("section", None, "latent"), P("section", None, "latent")),
        check_vma=False,
    )
```

time: 297 us -> 87.4 us (0.29)
  the two profiles are of different devices: /device:TPU:16 before, /device:TPU:1 now
where the time goes in v1:
time: 87.4 us; the launch traced here: 87.2 us
  Pallas kernels  79.6 us (91%)
  local copies, waits for them, and re-layouts  6.94 us (8%)
    pallas_call x1, Pallas kernels, shards(): pl.pallas_call(kernel, out_shape=(jax.ShapeDtypeStruct((1, tokens // GROU...  79.6 us
    unnamed x11, local copies, waits for them, and re-layouts  6.22 us

profile of v1, /device:TPU:1, one launch (start us, length us, event | category | flops | bytes accessed | tf_op | source)
XLA Modules:
  0.0 87.2 jit_solution(5462245496318084772)
XLA Ops:
  0.6 0.0 copy-start
  0.6 2.0 %copy-done = bf16[1,3,128,4608]{3,2,1,0:T(8,128)(2,1)S(1)} copy-done((bf16[1,3,128,4608]{3,2,1,0:T(8,128)(2,1)S(1)}, bf16[1,3,128,4608]{3,2,1,0:T(8,128)(2,1)}, u32[]{:S(2)}) %copy-start) | copy-done | bytes 3538968
  2.6 0.0 copy-start.1
  2.6 1.3 %copy-done.1 = bf16[1,4608,128]{2,1,0:T(8,128)(2,1)S(1)} copy-done((bf16[1,4608,128]{2,1,0:T(8,128)(2,1)S(1)}, bf16[1,4608,128]{2,1,0:T(8,128)(2,1)}, u32[]{:S(2)}) %copy-start.1) | copy-done | bytes 1179672
  3.9 0.0 copy-start.2
  3.9 1.0 %copy-done.2 = bf16[4,320,144]{1,2,0:T(8,128)(2,1)S(1)} copy-done((bf16[4,320,144]{1,2,0:T(8,128)(2,1)S(1)}, bf16[4,320,144]{1,2,0:T(8,128)(2,1)}, u32[]{:S(2)}) %copy-start.2) | copy-done | bytes 368664
  4.9 0.0 copy-start.3
  4.9 0.7 copy-done.3
  5.6 0.0 copy-start.4
  5.6 0.7 copy-done.4
  6.2 79.6 %shard_map.68 = (bf16[1,80,144]{2,1,0:T(8,128)(2,1)S(1)}, bf16[1,320,128]{2,1,0:T(8,128)(2,1)S(1)}) custom-call(bf16[4,144,320]{2,1,0:T(8,128)(2,1)S(1)} %bitcast.1, bf16[1,4608,128]{2,1,0:T(8,128)(2,1)S(1)} %copy-done.1, f32[1,128]{1,0:T(1,128)S(1)} %copy-done.3, s32[1,128]{1,0:T(1,128)S(1)} %copy-done.4, bf16[1,3,128,4608]{3,2,1,0:T(8,128)(2,1)S(1)} %copy-done), custom_call_target="tpu_custom_call" | custom-call | tf_op jit(solution)/shard_map/pallas_call | solution.py:255
  85.8 0.7 copy.7
  86.6 0.6 copy.9
Async XLA Ops:
  0.6 2.0 %copy-start = (bf16[1,3,128,4608]{3,2,1,0:T(8,128)(2,1)S(1)}, bf16[1,3,128,4608]{3,2,1,0:T(8,128)(2,1)}, u32[]{:S(2)}) copy-start(bf16[1,3,128,4608]{3,2,1,0:T(8,128)(2,1)} %dec.1) | copy-start | bytes 10616836
  2.6 1.3 %copy-start.1 = (bf16[1,4608,128]{2,1,0:T(8,128)(2,1)S(1)}, bf16[1,4608,128]{2,1,0:T(8,128)(2,1)}, u32[]{:S(2)}) copy-start(bf16[1,4608,128]{2,1,0:T(8,128)(2,1)} %enc.1) | copy-start | bytes 3538948
  3.9 1.0 %copy-start.2 = (bf16[4,320,144]{1,2,0:T(8,128)(2,1)S(1)}, bf16[4,320,144]{1,2,0:T(8,128)(2,1)}, u32[]{:S(2)}) copy-start(bf16[4,320,144]{1,2,0:T(8,128)(2,1)} %param.5) | copy-start | bytes 1105924
  4.9 0.7 copy-start.3
  5.6 0.7 copy-start.4

commit v2 on v0

v2 whole, which is shorter than its diff:
```python
import jax
import jax.numpy as jnp
from jax import lax
from jax.experimental import pallas as pl
from jax.experimental.pallas import tpu as pltpu
from jax.sharding import PartitionSpec as P

MESH = pl.DeviceIdType.MESH
BF16 = jnp.bfloat16
F32 = jnp.float32

NY = 8
GROUP = 4
LANES = 128
OFFSETS = (4, 3, -3, 2, -2, 1, -1, 0)
PLACE = {offset: place for place, offset in enumerate(OFFSETS)}
PLACE[-4] = PLACE[4]
TILES = ((0, 1), (2, 3), (4,))
FAR = (0, 1, 0, 1, 0)
FIRST = (0, 128, 256)
COUNT = (128, 128, 64)
PIECES = (
    (0, 0, 0, 80, 0),
    (0, 1, 80, 48, 0),
    (1, 1, 128, 32, 48),
    (1, 2, 160, 80, 0),
    (1, 3, 240, 16, 0),
    (2, 3, 256, 64, 16),
)


def kernel(
    resid, enc, bias, gate, dec, rec_out, act_out,
    resid_v, bias_v, gate_v, last_out, last_in, gathered, enc_v, dec_v, enc_t, dec_t, acts_in, acts_all,
    shares, sibling_in, ring, own_sum, final_out, final_in,
    load_sem, cross_send, cross_recv, gather_send, gather_recv, pair_send, pair_recv,
    act_send, act_recv, share_send, share_recv, ring_send, ring_recv, final_send, final_recv,
):
    width = gathered.shape[3]
    section = lax.axis_index("section")
    latent = lax.axis_index("latent")
    x_lo, z = section // 8, section % 8
    x_hi, y, core = latent // 16, latent // 2 % 8, latent % 2
    layer, g = section // GROUP, section % GROUP
    half = (x_hi, 1 - x_hi)

    def device(section_index, hi, y_index, core_index):
        return (section_index, hi * 16 + y_index * 2 + core_index)

    ways = (device(section, x_hi, (y + 1) % NY, core), device(section, x_hi, (y + NY - 1) % NY, core))
    sibling = device(section, x_hi, y, 1 - core)
    across = device((1 - x_lo) * 8 + z, 1 - x_hi, y, core)
    later = [((section + 4) % 16, latent), ((section + 8) % 16, latent)]
    partners = [*ways, sibling, across, later[0], later[1], ((section + 12) % 16, latent)]
    for turn in range(GROUP):
        for q in range(2):
            if turn or q:
                partners.append(device(section - g + (g + turn) % GROUP, half[q], y, core))
    barrier = pltpu.get_barrier_semaphore()
    for partner in partners:
        pl.semaphore_signal(barrier, inc=1, device_id=partner, device_id_type=MESH)
    loads = [
        pltpu.make_async_copy(resid.at[layer], resid_v.at[0], load_sem.at[0]),
        pltpu.make_async_copy(resid.at[(1 - x_lo) * 2 + z // 4], resid_v.at[1], load_sem.at[1]),
        pltpu.make_async_copy(enc.at[0], enc_v, load_sem.at[2]),
        pltpu.make_async_copy(dec.at[0], dec_v, load_sem.at[3]),
        pltpu.make_async_copy(bias, bias_v, load_sem.at[4]),
        pltpu.make_async_copy(gate, gate_v, load_sem.at[5]),
    ]
    for load in loads:
        load.start()

    def remote(source, target, send, recv, to):
        copy = pltpu.make_async_remote_copy(
            src_ref=source, dst_ref=target, send_sem=send, recv_sem=recv, device_id=to, device_id_type=MESH
        )
        copy.start()
        return copy

    loads[0].wait()
    loads[1].wait()
    for chunk in range(2):
        gathered[2 * chunk + x_hi, y, core] = resid_v[0, :, chunk * LANES : (chunk + 1) * LANES]
    last_out[:, 0:64] = resid_v[1, :, 256:320]
    last_out[:, 64:128] = resid_v[1, :, 256:320]
    pl.semaphore_wait(barrier, len(partners))

    gather, pairs = {}, {}
    units = ((0, 1), (2, 3), (4,))

    def tile_of(unit):
        return 4 if unit == 4 else unit // 2 * 2 + half[unit % 2]

    def around(offset):
        return (y + (offset + NY) % NY) % NY

    def send_gather(step, way, unit):
        block = gathered.at[tile_of(unit), around(-step if way == 0 else step), core]
        gather[step, way, unit] = remote(
            block, block, gather_send.at[step, way, unit], gather_recv.at[step, way, unit], ways[way]
        )

    def send_pair(offset, unit):
        block = gathered.at[tile_of(unit), around(offset), core]
        place = PLACE[offset]
        pairs[place, unit] = remote(block, block, pair_send.at[place, unit], pair_recv.at[place, unit], sibling)

    crossed = []
    for chunk in range(2):
        crossed.append(
            remote(
                resid_v.at[1, :, pl.ds(chunk * LANES, LANES)],
                gathered.at[2 * chunk + x_hi, y, core],
                cross_send.at[chunk],
                cross_recv.at[chunk],
                across,
            )
        )
    crossed.append(remote(last_out, last_in, cross_send.at[2], cross_recv.at[2], across))
    for chunk in range(2):
        for way in range(2):
            send_gather(0, way, 2 * chunk)
        send_pair(0, 2 * chunk)

    loads[2].wait()

    def turn_encoder(block, carry):
        rows = pl.ds(pl.multiple_of(block * 2 * width, 16), 2 * width)
        enc_t[block] = jnp.transpose(enc_v[rows, :])
        return carry

    lax.fori_loop(0, 8, turn_encoder, 0)
    for chunk in range(2):
        crossed[chunk].wait_recv()
        for way in range(2):
            send_gather(0, way, 2 * chunk + 1)
        send_pair(0, 2 * chunk + 1)
    crossed[2].wait_recv()
    own_last, other_last = resid_v[0, :, 256:320], last_in[:, 0:64]
    is_low = x_hi == 0
    gathered[4, y, core] = jnp.concatenate(
        [jnp.where(is_low, own_last, other_last), jnp.where(is_low, other_last, own_last)], axis=1
    )
    for way in range(2):
        send_gather(0, way, 4)
    send_pair(0, 4)
    lax.fori_loop(8, 16, turn_encoder, 0)
    for load in loads[3:]:
        load.wait()

    def turn_decoder(block, carry):
        columns = pl.ds(pl.multiple_of(block * 128, 128), 128)
        for k in range(3):
            dec_t[columns, k * 128 : (k + 1) * 128] = jnp.transpose(dec_v[k, :, columns])
        return carry

    def receive(chunk, step):
        for unit in units[chunk]:
            far = unit % 2
            for way in range(2):
                if (step, way, unit) not in gather:
                    continue
                gather[step, way, unit].wait_recv()
                if step < 2 or (step == 2 and way == far):
                    send_gather(step + 1, way, unit)
                send_pair((step + 1) * (-1 if way == 0 else 1), unit)

    preacts = {}

    def encode(chunk, offset):
        origin = around(offset)
        for unit in units[chunk]:
            pairs[PLACE[offset], unit].wait_recv()
        for hi in range(2):
            block = gathered[TILES[chunk][hi] if chunk < 2 else 4, origin].reshape(2 * width, LANES)
            term = jnp.dot(enc_t[hi * NY + origin], block, preferred_element_type=F32)
            key = (chunk, hi if chunk == 2 else 0)
            preacts[key] = term if key not in preacts else preacts[key] + term

    passed = {}

    def activate(chunk):
        first, count = FIRST[chunk], COUNT[chunk]
        preact = jnp.transpose(preacts[chunk, 0])
        if chunk == 2:
            preact = preact[0:64] + jnp.transpose(preacts[2, 1])[64:128]
        preact = preact + bias_v[...]
        threshold = 10000.0 * (gate_v[...].astype(F32) - 1.0)
        acts = jnp.where(preact > threshold, preact, jnp.zeros_like(preact)).astype(BF16)
        act_out[0, first : first + count] = acts
        rows = pl.ds(first, count)
        for k in range(2):
            passed[chunk, k] = remote(
                act_out.at[0, rows], acts_in.at[k, rows], act_send.at[chunk, k], act_recv.at[chunk, k], later[k]
            )
        fill(chunk, 0, acts)

    def fill(chunk, k, acts):
        first, count = FIRST[chunk], COUNT[chunk]
        acts_all[first : first + count, k * 128 : (k + 1) * 128] = acts
        if chunk == 2:
            acts_all[320:384, k * 128 : (k + 1) * 128] = acts

    def take(chunk):
        first, count = FIRST[chunk], COUNT[chunk]
        for k in range(2):
            passed[chunk, k].wait_recv()
            arrived = acts_in[k, first : first + count]
            fill(chunk, k + 1, jnp.where(layer > k, arrived, jnp.zeros_like(arrived)))

    share_copies, ring_copies = {}, {}

    def decode(chunk, place):
        target = around(OFFSETS[place])

        def product(hi):
            rows = pl.ds(pl.multiple_of((hi * NY + target) * 2 * width, 16), 2 * width)
            return lax.dot_general(
                dec_t[rows, :],
                acts_all[chunk * LANES : (chunk + 1) * LANES],
                (((1,), (1,)), ((), ())),
                preferred_element_type=F32,
            )

        if chunk == 2:
            lane = lax.broadcasted_iota(jnp.int32, (2 * width, LANES), 1)
            shares[place, 4] = jnp.where(lane < 64, product(0), product(1)).astype(BF16).reshape(2, width, LANES)
        else:
            for hi in range(2):
                shares[place, TILES[chunk][hi]] = product(hi).astype(BF16).reshape(2, width, LANES)
        for tile in TILES[chunk]:
            share_copies[place, tile] = remote(
                shares.at[place, tile, 1 - core],
                sibling_in.at[place, tile],
                share_send.at[place, tile],
                share_recv.at[place, tile],
                sibling,
            )

    def chip_sum(place, tile):
        share_copies[place, tile].wait_recv()
        return shares[place, tile, core].astype(F32) + sibling_in[place, tile].astype(F32)

    def add_ring(way, distance, tile):
        total = chip_sum(PLACE[distance if way == 0 else -distance], tile)
        if (way, distance + 1, tile) in ring_copies:
            ring_copies[way, distance + 1, tile].wait_recv()
            total = total + ring[way, distance, tile].astype(F32)
        ring[way, distance, tile] = total.astype(BF16)
        ring_copies[way, distance, tile] = remote(
            ring.at[way, distance, tile],
            ring.at[way, distance - 1, tile],
            ring_send.at[way, distance, tile],
            ring_recv.at[way, distance, tile],
            ways[way],
        )

    def add_far(chunk):
        for tile in TILES[chunk]:
            add_ring(FAR[tile], 4, tile)

    def add_near(chunk):
        for tile in TILES[chunk]:
            add_ring(1 - FAR[tile], 3, tile)

    def add_third(chunk):
        for tile in TILES[chunk]:
            add_ring(FAR[tile], 3, tile)

    def add_both(chunk, distance):
        for tile in TILES[chunk]:
            for way in range(2):
                add_ring(way if tile % 2 else 1 - way, distance, tile)

    always, others = [], []

    def finish(chunk):
        first, count = FIRST[chunk], COUNT[chunk]
        for tile in TILES[chunk]:
            total = chip_sum(7, tile)
            for way in range(2):
                ring_copies[way, 1, tile].wait_recv()
                total = total + ring[way, 0, tile].astype(F32)
            turned = jnp.transpose(total)
            parts = ((0, turned[0:64]), (1, turned[64:128])) if chunk == 2 else ((tile % 2, turned),)
            for hi, part in parts:
                own_sum[hi, first : first + count] = part
                final_out[hi, first : first + count] = part.astype(BF16)
        for index, (piece_chunk, target, token, rows, row) in enumerate(PIECES):
            if piece_chunk != chunk:
                continue

            def copy_to(q, index=index, target=target, token=token, rows=rows, row=row):
                return pltpu.make_async_remote_copy(
                    src_ref=final_out.at[half[q], pl.ds(token, rows)],
                    dst_ref=final_in.at[q * GROUP + g, pl.ds(row, rows)],
                    send_sem=final_send.at[index, q],
                    recv_sem=final_recv.at[index, q * GROUP + g],
                    device_id=device(section - g + target, half[q], y, core),
                    device_id_type=MESH,
                )

            far = copy_to(1)
            far.start()
            always.append(far)
            near = copy_to(0)
            others.append((target, near))

            @pl.when(g != target)
            def _(near=near):
                near.start()

    def collect(index):
        _, target, token, rows, row = PIECES[index]

        @pl.when(g == target)
        def _():
            total = own_sum[x_hi, token : token + rows]
            for q in range(2):
                for source in range(GROUP):
                    if q == 0 and source == target:
                        continue
                    slot = q * GROUP + source
                    arrived = final_in.at[slot, pl.ds(row, rows)]
                    pltpu.make_async_remote_copy(
                        src_ref=arrived,
                        dst_ref=arrived,
                        send_sem=final_send.at[index, q],
                        recv_sem=final_recv.at[index, slot],
                        device_id=device(section - g + source, half[q], y, core),
                        device_id_type=MESH,
                    ).wait_recv()
                    total = total + final_in[slot, row : row + rows].astype(F32)
            rec_out[0, row : row + rows] = total.astype(BF16)

    turned_to = [0]

    def turn_some(count):
        stop = min(36, turned_to[0] + count)
        lax.fori_loop(turned_to[0], stop, turn_decoder, 0)
        turned_to[0] = stop

    turn_some(4)
    receive(0, 0)
    receive(1, 0)
    encode(0, 0)
    encode(1, 0)
    receive(2, 0)
    turn_some(4)
    receive(0, 1)
    receive(1, 1)
    for chunk in range(2):
        encode(chunk, 1)
        encode(chunk, -1)
    receive(2, 1)
    turn_some(8)
    encode(2, 0)
    receive(0, 2)
    encode(0, 2)
    encode(0, -2)
    receive(1, 2)
    encode(1, 2)
    encode(1, -2)
    receive(2, 2)
    turn_some(8)
    encode(0, 3)
    encode(0, -3)
    receive(0, 3)
    encode(1, 3)
    encode(1, -3)
    encode(0, 4)
    activate(0)
    receive(1, 3)
    turn_some(4)
    encode(1, 4)
    activate(1)
    for offset in (1, -1, 2, -2, 3, -3):
        encode(2, offset)
    receive(2, 3)
    encode(2, 4)
    activate(2)
    turn_some(36)

    take(0)
    decode(0, 0)
    decode(0, 1)
    add_far(0)
    decode(0, 2)
    add_near(0)
    decode(0, 3)
    decode(0, 4)
    add_third(0)
    take(1)
    decode(1, 0)
    decode(1, 1)
    add_far(1)
    decode(1, 2)
    add_near(1)
    decode(0, 5)
    decode(0, 6)
    add_both(0, 2)
    decode(1, 3)
    decode(1, 4)
    add_third(1)
    take(2)
    decode(2, 0)
    decode(2, 1)
    add_far(2)
    decode(2, 2)
    add_near(2)
    decode(0, 7)
    add_both(0, 1)
    decode(1, 5)
    decode(1, 6)
    add_both(1, 2)
    decode(2, 3)
    decode(2, 4)
    add_third(2)
    decode(1, 7)
    finish(0)
    add_both(1, 1)
    decode(2, 5)
    decode(2, 6)
    add_both(2, 2)
    decode(2, 7)
    finish(1)
    add_both(2, 1)
    finish(2)
    for index in range(len(PIECES)):
        collect(index)

    for group in (crossed, gather.values(), pairs.values(), passed.values(), share_copies.values(), ring_copies.values(), always):
        for copy in group:
            copy.wait_send()
    for target, near in others:

        @pl.when(g != target)
        def _(near=near):
            near.wait_send()


def shards(residual, encoder, enc_bias, gate_code, decoder):
    layers, tokens, width = residual.shape
    model = encoder.shape[1]
    vmem = pl.BlockSpec(memory_space=pltpu.VMEM)
    hbm = pl.BlockSpec(memory_space=pltpu.HBM)
    dma = pltpu.SemaphoreType.DMA
    return pl.pallas_call(
        kernel,
        out_shape=(
            jax.ShapeDtypeStruct((1, tokens // GROUP, width), BF16),
            jax.ShapeDtypeStruct((1, tokens, 128), BF16),
        ),
        in_specs=[hbm] * 5,
        out_specs=(vmem, vmem),
        scratch_shapes=[
            pltpu.VMEM((2, width, tokens), BF16),
            pltpu.VMEM((1, 128), F32),
            pltpu.VMEM((1, 128), jnp.int32),
            pltpu.VMEM((width, LANES), BF16),
            pltpu.VMEM((width, LANES), BF16),
            pltpu.VMEM((5, NY, 2, width, LANES), BF16),
            pltpu.VMEM((model, 128), BF16),
            pltpu.VMEM((3, 128, model), BF16),
            pltpu.VMEM((16, 128, 2 * width), BF16),
            pltpu.VMEM((model, 384), BF16),
            pltpu.VMEM((2, tokens, 128), BF16),
            pltpu.VMEM((384, 384), BF16),
            pltpu.VMEM((8, 5, 2, width, LANES), BF16),
            pltpu.VMEM((8, 5, width, LANES), BF16),
            pltpu.VMEM((2, 5, 5, width, LANES), BF16),
            pltpu.VMEM((2, tokens, width), F32),
            pltpu.VMEM((2, tokens, width), BF16),
            pltpu.VMEM((8, tokens // GROUP, width), BF16),
            dma((6,)),
            dma((3,)),
            dma((3,)),
            dma((4, 2, 5)),
            dma((4, 2, 5)),
            dma((8, 5)),
            dma((8, 5)),
            dma((3, 2)),
            dma((3, 2)),
            dma((8, 5)),
            dma((8, 5)),
            dma((2, 5, 5)),
            dma((2, 5, 5)),
            dma((len(PIECES), 2)),
            dma((len(PIECES), 2 * GROUP)),
        ],
        compiler_params=pltpu.CompilerParams(
            collective_id=0, has_side_effects=True, vmem_limit_bytes=60 * 1024 * 1024
        ),
    )(jnp.transpose(residual, (0, 2, 1)), encoder, enc_bias, gate_code, decoder)


def solution(mesh):
    return jax.shard_map(
        shards,
        mesh=mesh,
        in_specs=(
            P(None, None, "latent"),
            P("section", None, "latent"),
            P("section", "latent"),
            P("section", "latent"),
            P("section", None, "latent", None),
        ),
        out_specs=(P("section", None, "latent"), P("section", None, "latent")),
        check_vma=False,
    )
```

time: 297 us -> 76.1 us (0.26)
  the two profiles are of different devices: /device:TPU:16 before, /device:TPU:192 now
where the time goes in v2:
time: 76.1 us; the launch traced here: 75.9 us
  Pallas kernels  72.2 us (95%)
  local copies, waits for them, and re-layouts  3.02 us (4%)
    pallas_call x1, Pallas kernels, shards(): pl.pallas_call(kernel, out_shape=(jax.ShapeDtypeStruct((1, tokens // GROU...  72.2 us
    unnamed x1, local copies, waits for them, and re-layouts  1.53 us

profile of v2, /device:TPU:192, one launch (start us, length us, event | category | flops | bytes accessed | tf_op | source)
XLA Modules:
  0.0 75.9 jit_solution(4733620817828716319)
XLA Ops:
  0.6 72.2 %shard_map.68 = (bf16[1,80,144]{2,1,0:T(8,128)(2,1)}, bf16[1,320,128]{2,1,0:T(8,128)(2,1)}) custom-call(bf16[4,144,320]{2,1,0:T(8,128)(2,1)} %bitcast.1, bf16[1,4608,128]{2,1,0:T(8,128)(2,1)} %enc.1, f32[1,128]{1,0:T(1,128)} %bias.1, s32[1,128]{1,0:T(1,128)} %gate.1, bf16[1,3,128,4608]{3,2,1,0:T(8,128)(2,1)} %dec.1), custom_call_target="tpu_custom_call" | custom-call | tf_op jit(solution)/shard_map/pallas_call | solution.py:448
  72.8 1.5 %copy.7 = bf16[1,80,144]{1,2,0:T(8,128)(2,1)} copy(bf16[1,80,144]{2,1,0:T(8,128)(2,1)} %get-tuple-element.2) | data formatting | bytes 46080 | tf_op jit(solution)/shard_map/pallas_call | solution.py:448
  74.3 1.5 %copy.9 = bf16[1,320,128]{2,1,0:T(8,128)(2,1)} copy(bf16[1,320,128]{2,1,0:T(8,128)(2,1)} %get-tuple-element.7) | data formatting | bytes 163840

commit v3 on v2

--- a/solution.py
+++ b/solution.py
@@ -83,7 +83,23 @@
         gathered[2 * chunk + x_hi, y, core] = resid_v[0, :, chunk * LANES : (chunk + 1) * LANES]
     last_out[:, 0:64] = resid_v[1, :, 256:320]
     last_out[:, 64:128] = resid_v[1, :, 256:320]
+    def turn_encoder(block, carry):
+        rows = pl.ds(pl.multiple_of(block * 2 * width, 16), 2 * width)
+        enc_t[block] = jnp.transpose(enc_v[rows, :])
+        return carry
+
+    loads[2].wait()
+    lax.fori_loop(0, 16, turn_encoder, 0)
+    for load in loads[3:]:
+        load.wait()
     pl.semaphore_wait(barrier, len(partners))
+
+    def turn_decoder(block, carry):
+        columns = pl.ds(pl.multiple_of(block * 128, 128), 128)
+        for k in range(3):
+            dec_t[columns, k * 128 : (k + 1) * 128] = jnp.transpose(dec_v[k, :, columns])
+        return carry
+
 
     gather, pairs = {}, {}
     units = ((0, 1), (2, 3), (4,))
@@ -122,14 +138,6 @@
             send_gather(0, way, 2 * chunk)
         send_pair(0, 2 * chunk)
 
-    loads[2].wait()
-
-    def turn_encoder(block, carry):
-        rows = pl.ds(pl.multiple_of(block * 2 * width, 16), 2 * width)
-        enc_t[block] = jnp.transpose(enc_v[rows, :])
-        return carry
-
-    lax.fori_loop(0, 8, turn_encoder, 0)
     for chunk in range(2):
         crossed[chunk].wait_recv()
         for way in range(2):
@@ -144,15 +152,6 @@
     for way in range(2):
         send_gather(0, way, 4)
     send_pair(0, 4)
-    lax.fori_loop(8, 16, turn_encoder, 0)
-    for load in loads[3:]:
-        load.wait()
-
-    def turn_decoder(block, carry):
-        columns = pl.ds(pl.multiple_of(block * 128, 128), 128)
-        for k in range(3):
-            dec_t[columns, k * 128 : (k + 1) * 128] = jnp.transpose(dec_v[k, :, columns])
-        return carry
 
     def receive(chunk, step):
         for unit in units[chunk]:
@@ -439,13 +438,18 @@
             near.wait_send()
 
 
+def hand_over(sums, acts, turned, copied):
+    turned[0] = jnp.transpose(sums[0])
+    copied[...] = acts[...]
+
+
 def shards(residual, encoder, enc_bias, gate_code, decoder):
     layers, tokens, width = residual.shape
     model = encoder.shape[1]
     vmem = pl.BlockSpec(memory_space=pltpu.VMEM)
     hbm = pl.BlockSpec(memory_space=pltpu.HBM)
     dma = pltpu.SemaphoreType.DMA
-    return pl.pallas_call(
+    sums, acts = pl.pallas_call(
         kernel,
         out_shape=(
             jax.ShapeDtypeStruct((1, tokens // GROUP, width), BF16),
@@ -492,6 +496,16 @@
             collective_id=0, has_side_effects=True, vmem_limit_bytes=60 * 1024 * 1024
         ),
     )(jnp.transpose(residual, (0, 2, 1)), encoder, enc_bias, gate_code, decoder)
+    turned, copied = pl.pallas_call(
+        hand_over,
+        out_shape=(
+            jax.ShapeDtypeStruct((1, width, tokens // GROUP), BF16),
+            jax.ShapeDtypeStruct((1, tokens, 128), BF16),
+        ),
+        in_specs=[vmem, vmem],
+        out_specs=(vmem, vmem),
+    )(sums, acts)
+    return jnp.transpose(turned, (0, 2, 1)), copied
 
 
 def solution(mesh):

time: 76.1 us -> 74.2 us (0.975)
  local copies, waits for them, and re-layouts: 3.02 us -> 0 us
  Pallas kernels: 72.2 us -> 73.4 us
    pallas_call x0 -> x1, Pallas kernels: none -> 1.6 us  [shards(): pl.pallas_call(hand_over, out_shape=(jax.ShapeDtypeStruct((1, width, toke...]
    unnamed x1 -> x0, local copies, waits for them, and re-layouts: 1.53 us -> none
    pallas_call x1 -> x0, local copies, waits for them, and re-layouts: 1.5 us -> none  [shards(): pl.pallas_call(kernel, out_shape=(jax.ShapeDtypeStruct((1, tokens // GROU...]
where the time goes in v3:
time: 74.2 us; the launch traced here: 74 us
  Pallas kernels  73.4 us (99%)
    pallas_call x1, Pallas kernels, shards(): pl.pallas_call(kernel, out_shape=(jax.ShapeDtypeStruct((1, tokens // GROU...  71.8 us
    pallas_call x1, Pallas kernels, shards(): pl.pallas_call(hand_over, out_shape=(jax.ShapeDtypeStruct((1, width, toke...  1.6 us

profile of v3, /device:TPU:192, one launch (start us, length us, event | category | flops | bytes accessed | tf_op | source)
XLA Modules:
  0.0 74.0 jit_solution(12733251419424571439)
XLA Ops:
  0.6 71.8 %shard_map.68 = (bf16[1,80,144]{2,1,0:T(8,128)(2,1)}, bf16[1,320,128]{2,1,0:T(8,128)(2,1)}) custom-call(bf16[4,144,320]{2,1,0:T(8,128)(2,1)} %bitcast.2, bf16[1,4608,128]{2,1,0:T(8,128)(2,1)} %enc.1, f32[1,128]{1,0:T(1,128)} %bias.1, s32[1,128]{1,0:T(1,128)} %gate.1, bf16[1,3,128,4608]{3,2,1,0:T(8,128)(2,1)} %dec.1), custom_call_target="tpu_custom_call" | custom-call | tf_op jit(solution)/shard_map/pallas_call | solution.py:452
  72.4 1.6 %shard_map.69 = (bf16[1,144,80]{2,1,0:T(8,128)(2,1)}, bf16[1,320,128]{2,1,0:T(8,128)(2,1)}) custom-call(bf16[1,80,144]{2,1,0:T(8,128)(2,1)} %get-tuple-element.6.sums, bf16[1,320,128]{2,1,0:T(8,128)(2,1)} %get-tuple-element.7.acts), custom_call_target="tpu_custom_call" | custom-call | tf_op jit(solution)/shard_map/pallas_call | solution.py:499

commit v4 on v3

--- a/solution.py
+++ b/solution.py
@@ -389,15 +389,15 @@
     decode(0, 3)
     decode(0, 4)
     add_third(0)
+    decode(0, 5)
+    decode(0, 6)
     take(1)
     decode(1, 0)
     decode(1, 1)
     add_far(1)
+    add_both(0, 2)
     decode(1, 2)
     add_near(1)
-    decode(0, 5)
-    decode(0, 6)
-    add_both(0, 2)
     decode(1, 3)
     decode(1, 4)
     add_third(1)

time: 74.2 us -> 74.9 us (level)
    pallas_call x1, Pallas kernels: 71.8 us -> 72.5 us  [shards(): pl.pallas_call(kernel, out_shape=(jax.ShapeDtypeStruct((1, tokens // GROU...]
where the time goes in v4:
time: 74.9 us; the launch traced here: 74.8 us
  Pallas kernels  74.1 us (99%)
    pallas_call x1, Pallas kernels, shards(): pl.pallas_call(kernel, out_shape=(jax.ShapeDtypeStruct((1, tokens // GROU...  72.5 us
    pallas_call x1, Pallas kernels, shards(): pl.pallas_call(hand_over, out_shape=(jax.ShapeDtypeStruct((1, width, toke...  1.6 us

profile of v4, /device:TPU:192, one launch (start us, length us, event | category | flops | bytes accessed | tf_op | source)
XLA Modules:
  0.0 74.8 jit_solution(7350471244322998700)
XLA Ops:
  0.6 72.5 %shard_map.68 = (bf16[1,80,144]{2,1,0:T(8,128)(2,1)}, bf16[1,320,128]{2,1,0:T(8,128)(2,1)}) custom-call(bf16[4,144,320]{2,1,0:T(8,128)(2,1)} %bitcast.2, bf16[1,4608,128]{2,1,0:T(8,128)(2,1)} %enc.1, f32[1,128]{1,0:T(1,128)} %bias.1, s32[1,128]{1,0:T(1,128)} %gate.1, bf16[1,3,128,4608]{3,2,1,0:T(8,128)(2,1)} %dec.1), custom_call_target="tpu_custom_call" | custom-call | tf_op jit(solution)/shard_map/pallas_call | solution.py:452
  73.2 1.6 %shard_map.69 = (bf16[1,144,80]{2,1,0:T(8,128)(2,1)}, bf16[1,320,128]{2,1,0:T(8,128)(2,1)}) custom-call(bf16[1,80,144]{2,1,0:T(8,128)(2,1)} %get-tuple-element.6.sums, bf16[1,320,128]{2,1,0:T(8,128)(2,1)} %get-tuple-element.7.acts), custom_call_target="tpu_custom_call" | custom-call | tf_op jit(solution)/shard_map/pallas_call | solution.py:499
